TPU v7x, 256 devices: a whole 4x4x8 slice. The times are simulated.
256 devices in a mesh: kx: 8 (over z), ht: 8 (over y, core), real: 4 (over x).
Axes of the slice: x: 4, y: 4, z: 8, core: 2. Of those that a mesh axis runs over, the one named last changes fastest.
Arguments:
- velocity: float32 [3, 4, 32, 512, 128], P(None, 'real', 'kx', 'ht'), may hold values from -6 to 6
- low_index: int32 [8], replicated, may hold values from 0 to 31, as said below
- neighbours: int32 [32, 8], P('kx'), may hold values from 0 to 31, as said below
- owner_map: int32 [64], replicated, may hold values from 0 to 63, each once
- mode_counts: int32 [32], P('kx'), may hold values from 16 to 64
- helmholtz: float32 [64, 512, 512], P(('kx', 'ht')), may hold values from -0.25 to 0.25
Outputs:
- velocity_next: float32 [3, 4, 32, 512, 128], P(None, 'real', 'kx', 'ht')
Inputs may be any that keep to these rules, and one draw needn't show every extreme that they name: `low_index`: distinct values. neighbours[m, j] lies within 4 modes of m, counting circularly over the 32 modes; offsets of + 4 and - 4 both occur.
All inputs are finite; a program needn't handle non-finite values.
Results may differ from a plain program's by a relative error of at most 0.0001.
Values sent between devices are 32-bit elements; how exact they have to be, the bound alone decides.
A program may use at most 64 MiB of HBM per device.

v0:
```python
import jax
import jax.numpy as jnp
from jax import lax
from jax.sharding import PartitionSpec as P

dt_step = 0.1


def extended_2(block, sides, width):
    for axis, dim in sides:
        count = lax.axis_size(axis)
        forward = [(i, i + 1) for i in range(count - 1)]
        forward.append((count - 1, 0))
        backward = [(target, source) for source, target in forward]
        low = lax.ppermute(
            lax.slice_in_dim(block, block.shape[dim] - width, None, axis=dim), axis, forward
        )
        high = lax.ppermute(lax.slice_in_dim(block, 0, width, axis=dim), axis, backward)
        block = jnp.concatenate([low, block, high], axis=dim)
    return block


def spanwise_tables(mode_count, point_count):
    column_ids = jnp.arange(2 * mode_count)
    wavenumber = (column_ids // 2).astype(jnp.float32)
    imag_part = column_ids % 2
    positions = 2.0 * jnp.pi * jnp.arange(point_count).astype(jnp.float32) / point_count
    phases = wavenumber[:, None] * positions[None, :]
    forward = jnp.where(imag_part[:, None] == 0, jnp.cos(phases), -jnp.sin(phases)) / jnp.sqrt(
        jnp.float32(mode_count)
    )
    backward = forward.T * (2.0 * mode_count / point_count)
    return (forward, backward)


def apply_inverse(block, helmholtz, kx_count, ht_count, slots_dev, rows_ht):
    components, reals_dev, band_modes = (block.shape[0], block.shape[1], block.shape[2])
    regrouped = block.reshape(
        components, reals_dev, band_modes, kx_count, ht_count, slots_dev, 2, rows_ht
    )
    regrouped = regrouped.transpose(0, 1, 3, 2, 5, 6, 4, 7)
    regrouped = regrouped.reshape(
        components, reals_dev, kx_count * band_modes, slots_dev, 2, ht_count * rows_ht
    )
    solved = jnp.einsum("syx,crmspx->crmspy", helmholtz, regrouped, precision=lax.Precision.HIGHEST)
    solved = solved.reshape(
        components, reals_dev, kx_count, band_modes, slots_dev, 2, ht_count, rows_ht
    )
    solved = solved.transpose(0, 1, 3, 2, 6, 4, 5, 7)
    return solved.reshape(block.shape)


def local(velocity, low_index, neighbours, owner_map, mode_counts, helmholtz):
    highest = lax.Precision.HIGHEST
    components, reals_dev, band_modes, rows_ht, columns = velocity.shape
    kz_modes = columns // 2
    forward, backward = spanwise_tables(kz_modes, 4 * kz_modes)
    kx_count = lax.axis_size("kx")
    ht_count = lax.axis_size("ht")
    kx_total = band_modes * kx_count
    realizations = reals_dev * lax.axis_size("real")
    owners = kx_count * ht_count
    slots_dev = kz_modes // owners
    width_out = slots_dev * 2 * rows_ht
    low_members = low_index.shape[0]
    band_start = lax.axis_index("kx") * band_modes
    global_modes = band_start + jnp.arange(band_modes, dtype=jnp.int32)
    low_select = (low_index[:, None] == global_modes[None, :]).astype(jnp.float32)
    high_mask = 1.0 - jnp.sum(low_select, axis=0)
    offsets = (neighbours - global_modes[:, None] + kx_total // 2) % kx_total - kx_total // 2
    local_partner = jnp.arange(band_modes, dtype=jnp.int32)[:, None] + band_modes + offsets
    column_mask = ((jnp.arange(columns) // 2)[None, :] < mode_counts[:, None]).astype(jnp.float32)
    inverse_map = (
        jnp.zeros((kz_modes,), jnp.int32).at[owner_map].set(jnp.arange(kz_modes, dtype=jnp.int32))
    )
    current = velocity
    physical = jnp.dot(current, forward, precision=highest)
    extended = extended_2(physical, (("kx", 2),), band_modes)
    own_low = jnp.einsum("jm,crmyz->crjyz", low_select, physical, precision=highest)
    low_fields = lax.psum(own_low, "kx")
    high_low = jnp.zeros_like(physical)
    stresses = []
    for member in range(low_members):
        partner = jnp.take(extended, local_partner[:, member], axis=2)
        low_one = low_fields[:, :, member : member + 1]
        high_low = high_low + low_one * partner[1:2] + partner * low_one[1:2]
        weighted = physical * (partner[1:2] * high_mask[None, None, :, None, None])
        stresses.append(jnp.sum(weighted, axis=(1, 2)))
    stress = jnp.stack(stresses, axis=1)
    nonlinear = jnp.dot(high_low, backward, precision=highest)
    summed = lax.psum(stress, ("kx", "real"))
    low_forcing = jnp.dot(summed / realizations, backward, precision=highest)
    forcing = nonlinear * high_mask[None, None, :, None, None]
    forcing = (
        forcing + jnp.einsum("jm,cjyk->cmyk", low_select, low_forcing, precision=highest)[:, None]
    )
    forcing = forcing * column_mask[None, None, :, None, :]
    updated = current + dt_step * forcing
    slotted = jnp.take(
        updated.reshape(components, reals_dev, band_modes, rows_ht, kz_modes, 2), owner_map, axis=4
    )
    outgoing = slotted.reshape(components, reals_dev, band_modes, rows_ht, owners, slots_dev, 2)
    outgoing = outgoing.transpose(0, 1, 2, 4, 5, 6, 3)
    flat_out = outgoing.reshape(components, reals_dev, band_modes, owners, width_out)
    applied = apply_inverse(
        lax.all_to_all(flat_out, ("kx", "ht"), split_axis=3, concat_axis=3, tiled=True),
        helmholtz,
        kx_count,
        ht_count,
        slots_dev,
        rows_ht,
    )
    returned = lax.all_to_all(applied, ("kx", "ht"), split_axis=3, concat_axis=3, tiled=True)
    restored = returned.reshape(components, reals_dev, band_modes, owners, slots_dev, 2, rows_ht)
    restored = restored.transpose(0, 1, 2, 6, 3, 4, 5).reshape(
        components, reals_dev, band_modes, rows_ht, kz_modes, 2
    )
    current = jnp.take(restored, inverse_map, axis=4).reshape(
        components, reals_dev, band_modes, rows_ht, columns
    )
    return current


def solution(mesh):
    in_specs = (
        P(None, "real", "kx", "ht", None),
        P(),
        P("kx", None),
        P(),
        P("kx"),
        P(("kx", "ht"), None, None),
    )
    out_specs = P(None, "real", "kx", "ht", None)
    return jax.shard_map(local, mesh=mesh, in_specs=in_specs, out_specs=out_specs, check_vma=False)
```

profile of v0, /device:TPU:1, one launch (start us, length us, event | category | flops | bytes accessed | tf_op | source)
XLA Modules:
  0.0 327.1 jit_solution(15920989410416831472)
XLA Ops:
  6.6 2.4 fusion.12
  9.0 2.5 collective-permute-start
  11.5 4.0 %collective-permute-start.1 = (f32[3,1,4,64,256]{4,3,2,0,1:T(8,128)S(1)}, f32[3,1,4,64,256]{4,3,2,0,1:T(8,128)}, u32[]{:S(2)}, u32[]{:S(2)}) collective-permute-start(f32[3,1,4,64,256]{4,3,2,0,1:T(8,128)S(1)} %bitcast.259), channel_id=1, source_target_pairs={{32,0},{64,32},{96,64},{128,96},{160,128},{192,160},{224,192},{0,2... | collective-permute-start | bytes 2359304 | tf_op jit(solution)/shard_map/ppermute | solution.py:18
  15.6 3.1 convolution_bitcast_fusion
  19.8 12.9 %collective-permute-done = f32[3,1,4,64,256]{4,3,2,0,1:T(8,128)S(1)} collective-permute-done((f32[3,1,4,64,256]{4,3,2,0,1:T(8,128)S(1)}, f32[3,1,4,64,256]{4,3,2,0,1:T(8,128)S(1)}, u32[]{:S(2)}, u32[]{:S(2)}) %collective-permute-start) | collective-permute-done | bytes 786464 | tf_op jit(solution)/shard_map/ppermute | solution.py:15
  33.6 1.8 maximum_bitcast_fusion
  35.4 1.6 gather_fusion.7
  37.0 1.5 gather_fusion.5
  38.5 1.5 gather_fusion.4
  40.0 1.5 gather_fusion.3
  41.5 1.5 gather_fusion.2
  43.0 1.5 gather_fusion.1
  46.0 1.5 gather_fusion.6
  55.4 3.9 %stack.35 = f32[3,8,64,256]{3,1,2,0:T(8,128)} concatenate(f32[3,1,64,256]{3,1,2,0:T(1,128)S(1)} %stack.27, f32[3,1,64,256]{3,1,2,0:T(1,128)S(1)} %stack.28, f32[3,1,64,256]{3,1,2,0:T(1,128)S(1)} %stack.29, f32[3,1,64,256]{3,1,2,0:T(1,128)S(1)} %stack.30, f32[3,1,64,256]{3,1,2,0:T(1,128)S(1)} %stack.31, f32[3,1,64,256]{3,1,2,0:T(1,128)S(1)} %stack.32, ...), dimensions={1} | concatenate | bytes 3145728 | tf_op jit(solution)/shard_map/stack | solution.py:89
  60.4 35.1 %all-reduce.3.cloned.1.call-done = f32[3,1,8,64,256]{4,2,3,0,1:T(8,128)} async-done(((f32[3,1,8,64,256]{4,2,3,0,1:T(8,128)}), f32[3,1,8,64,256]{4,2,3,0,1:T(8,128)}) %all-reduce.3.cloned.1.call-update) | async-done | bytes 1572880 | tf_op jit(solution)/shard_map/psum | solution.py:80
  95.5 7.7 %fusion.51 = (f32[3,1,1,64,256]{4,2,3,0,1:T(1,128)S(1)}, f32[3,1,1,64,256]{4,2,3,0,1:T(1,128)S(1)}, f32[3,1,1,64,256]{4,2,3,0,1:T(1,128)S(1)}, f32[3,1,1,64,256]...) fusion(f32[3,1,8,64,256]{4,2,3,0,1:T(8,128)} %all-reduce.3.clon, ...), kind=kLoop, calls=%fused_computation.172 | loop fusion | bytes 3145728 | tf_op jit(solution)/shard_map/slice | solution.py:85
  108.7 3.5 %fusion.52 = (f32[1,1,1,64,256]{4,2,3,0,1:T(1,128)S(1)}, f32[1,1,1,64,256]{4,2,3,0,1:T(1,128)S(1)}, f32[1,1,1,64,256]{4,2,3,0,1:T(1,128)S(1)}, f32[1,1,1,64,256]...) fusion(f32[3,1,8,64,256]{4,2,3,0,1:T(8,128)} %all-reduce.3.clon, ...), kind=kLoop, calls=%fused_computation.173 | loop fusion | bytes 1048576 | tf_op jit(solution)/shard_map/slice | solution.py:86
  116.0 133.7 %all-reduce.5.cloned.1.call-done = f32[3,8,64,256]{3,1,2,0:T(8,128)} async-done(((f32[3,8,64,256]{3,1,2,0:T(8,128)}), f32[3,8,64,256]{3,1,2,0:T(8,128)}) %all-reduce.5.cloned.1.call-update) | async-done | bytes 1572880 | tf_op jit(solution)/shard_map/psum | solution.py:91
  249.7 3.5 %fusion = f32[3,8,64,128]{3,1,2,0:T(8,128)S(1)} fusion(f32[3,8,64,256]{3,1,2,0:T(8,128)} %all-reduce.5.cloned.1.call-done, f32[256]{0:T(256)S(1)} %convert_multiply_fusion, f32[128]{0:T(128)} %copy-done.17, pred[128]{0:T(512)(128)(4,1)S(1)} %fusion.42), kind=kOutput, calls=%fused_computation.12 | convolution fusion | flops 604504064 | bytes 2360960 | tf_op jit(solution)/shard_map/dot_general | solution.py:92
  254.4 5.9 %fusion.6 = f32[3,1,4,64,128]{4,3,2,0,1:T(8,128)} fusion(f32[3,1,4,64,128]{4,3,2,1,0:T(8,128)S(1)} %copy-done.14, f32[3,64,128,4]{2,3,1,0:T(4,128)S(1)} %fusion.50, f32[4,128]{1,0:T(4,128)S(1)} %compare_convert_fusion.1, f32[4]{0:T(128)} %copy-done.27, f32[256]{0:T(256)S(1)} %convert_multiply_fusion, f32[128]{0:T(128)} %copy-done.17, ...), kind=kOutput, calls=%fused_computation.21 | convolution fusion | flops 310280192 | bytes 11669168 | tf_op jit(solution)/shard_map/dot_general | solution.py:90
  264.4 27.5 %all_to_all.10 = f32[3,1,4,64,128]{4,2,0,1,3:T(4,128)S(1)} all-to-all(f32[3,1,4,64,128]{4,2,0,1,3:T(4,128)S(1)} %reshape.457), channel_id=1, replica_groups=mesh['kx'=8,'ht'=8,'real'=4] {'kx','ht'}, dimensions={3} | all-to-all | bytes 786432 | tf_op jit(solution)/shard_map/all_to_all | solution.py:106
  292.8 1.5 convolution_bitcast_fusion.1
  296.2 5.5 %all-to-all-start.1 = ((f32[3,1,4,64,128]{4,2,0,1,3:T(4,128)}), f32[3,1,4,64,128]{4,2,0,1,3:T(4,128)S(1)}, u32[]{:S(2)}, u32[]{:S(2)}) async-start(f32[3,1,4,64,128]{4,2,0,1,3:T(4,128)} %reshape.459), calls=%async_computation.1 | async-start | bytes 786432 | tf_op jit(solution)/shard_map/all_to_all | solution.py:113
  302.6 14.2 %all-to-all-done.1 = f32[3,1,4,64,128]{4,2,0,1,3:T(4,128)S(1)} async-done(((f32[3,1,4,64,128]{4,2,0,1,3:T(4,128)}), f32[3,1,4,64,128]{4,2,0,1,3:T(4,128)S(1)}, u32[]{:S(2)}, u32[]{:S(2)}) %all-to-all-start.1) | async-done | bytes 393248 | tf_op jit(solution)/shard_map/all_to_all | solution.py:113
  (169 shorter events, 33.5 us)
Async XLA Ops:
  6.5 286.2 %copy-start = (f32[1,512,512]{2,1,0:T(8,128)S(1)}, f32[1,512,512]{2,1,0:T(8,128)}, u32[]{:S(2)}) copy-start(f32[1,512,512]{2,1,0:T(8,128)} %param.15) | copy-start | bytes 3145732
  6.5 89.0 %all-reduce.3.cloned.1.call-start = ((), (), s32[]{:S(2)}) async-start(), calls=%async_computation.2 | async-start | bytes 3145728 | tf_op jit(solution)/shard_map/psum | solution.py:80
  6.6 12.2 %copy-start.17 = (f32[128]{0:T(128)}, f32[128]{0:T(128)S(1)}, u32[]{:S(2)}) copy-start(f32[128]{0:T(128)S(1)} %fusion.45) | copy-start | bytes 1540
  6.6 12.2 %copy-start.28 = (s32[4,8]{1,0:T(4,128)S(1)}, s32[4,8]{1,0:T(4,128)}, u32[]{:S(2)}) copy-start(s32[4,8]{1,0:T(4,128)} %param.12) | copy-start | bytes 388
  6.6 13.0 %copy-start.29 = (s32[8]{0:T(128)S(1)}, s32[8]{0:T(128)}, u32[]{:S(2)}) copy-start(s32[8]{0:T(128)} %param.11) | copy-start | bytes 100
  9.0 23.7 %copy-start.1 = (f32[256,3,4,64]{0,3,2,1:T(8,128)}, f32[256,3,4,64]{0,3,2,1:T(8,128)S(1)}, u32[]{:S(2)}) copy-start(f32[256,3,4,64]{0,3,2,1:T(8,128)S(1)} %fusion.12) | copy-start | bytes 2359300
  9.0 23.7 %collective-permute-start = (f32[3,1,4,64,256]{4,3,2,0,1:T(8,128)S(1)}, f32[3,1,4,64,256]{4,3,2,0,1:T(8,128)S(1)}, u32[]{:S(2)}, u32[]{:S(2)}) collective-permute-start(f32[3,1,4,64,256]{4,3,2,0,1:T(8,128)S(1)} %bitcast.258), channel_id=1, source_target_pairs={{0,32},{32,64},{64,96},{96,128},{128,160},{160,192},{192,224},{224... | collective-permute-start | bytes 2359304 | tf_op jit(solution)/shard_map/ppermute | solution.py:15
  11.5 22.1 %collective-permute-start.1 = (f32[3,1,4,64,256]{4,3,2,0,1:T(8,128)S(1)}, f32[3,1,4,64,256]{4,3,2,0,1:T(8,128)}, u32[]{:S(2)}, u32[]{:S(2)}) collective-permute-start(f32[3,1,4,64,256]{4,3,2,0,1:T(8,128)S(1)} %bitcast.259), channel_id=1, source_target_pairs={{32,0},{64,32},{96,64},{128,96},{160,128},{192,160},{224,192},{0,2... | collective-permute-start | bytes 2359304 | tf_op jit(solution)/shard_map/ppermute | solution.py:18
  15.6 19.9 %copy-start.18 = (s32[4]{0:T(128)}, s32[4]{0:T(128)S(1)}, u32[]{:S(2)}) copy-start(s32[4]{0:T(128)S(1)} %get-tuple-element.70) | copy-start | bytes 52
  18.8 230.9 %all-reduce.5.cloned.1.call-start = ((), (), s32[]{:S(2)}) async-start(), calls=%async_computation.3 | async-start | bytes 3145728 | tf_op jit(solution)/shard_map/psum | solution.py:91
  19.2 28.2 %copy-start.19 = (pred[4]{0:T(512)(128)(4,1)}, pred[4]{0:T(512)(128)(4,1)S(1)}, u32[]{:S(2)}) copy-start(pred[4]{0:T(512)(128)(4,1)S(1)} %compare_and_fusion.2) | copy-start | bytes 16
  19.3 29.6 %copy-start.20 = (pred[4]{0:T(512)(128)(4,1)}, pred[4]{0:T(512)(128)(4,1)S(1)}, u32[]{:S(2)}) copy-start(pred[4]{0:T(512)(128)(4,1)S(1)} %compare_and_fusion.4) | copy-start | bytes 16
  19.3 30.9 %copy-start.21 = (pred[4]{0:T(512)(128)(4,1)}, pred[4]{0:T(512)(128)(4,1)S(1)}, u32[]{:S(2)}) copy-start(pred[4]{0:T(512)(128)(4,1)S(1)} %compare_and_fusion.5) | copy-start | bytes 16
  19.3 31.1 %copy-start.22 = (pred[4]{0:T(512)(128)(4,1)}, pred[4]{0:T(512)(128)(4,1)S(1)}, u32[]{:S(2)}) copy-start(pred[4]{0:T(512)(128)(4,1)S(1)} %compare_and_fusion.6) | copy-start | bytes 16
  19.4 31.2 %copy-start.23 = (pred[4]{0:T(512)(128)(4,1)}, pred[4]{0:T(512)(128)(4,1)S(1)}, u32[]{:S(2)}) copy-start(pred[4]{0:T(512)(128)(4,1)S(1)} %compare_and_fusion.7) | copy-start | bytes 16
  19.4 31.4 %copy-start.24 = (pred[4]{0:T(512)(128)(4,1)}, pred[4]{0:T(512)(128)(4,1)S(1)}, u32[]{:S(2)}) copy-start(pred[4]{0:T(512)(128)(4,1)S(1)} %compare_and_fusion.8) | copy-start | bytes 16
  19.7 31.8 %copy-start.25 = (pred[4]{0:T(512)(128)(4,1)}, pred[4]{0:T(512)(128)(4,1)S(1)}, u32[]{:S(2)}) copy-start(pred[4]{0:T(512)(128)(4,1)S(1)} %compare_and_fusion.9) | copy-start | bytes 16
  19.8 32.1 %copy-start.26 = (pred[4]{0:T(512)(128)(4,1)}, pred[4]{0:T(512)(128)(4,1)S(1)}, u32[]{:S(2)}) copy-start(pred[4]{0:T(512)(128)(4,1)S(1)} %compare_and_fusion.3) | copy-start | bytes 16
  19.8 32.3 %copy-start.27 = (f32[4]{0:T(128)}, f32[4]{0:T(128)S(1)}, u32[]{:S(2)}) copy-start(f32[4]{0:T(128)S(1)} %broadcast_subtract_fusion) | copy-start | bytes 52
  55.4 5.0 %copy-start.32 = (s32[4]{0:T(128)S(1)}, s32[4]{0:T(128)}, u32[]{:S(2)}) copy-start(s32[4]{0:T(128)} %param.14) | copy-start | bytes 52
  112.2 142.2 %copy-start.3 = (f32[4,3,64,256]{3,2,1,0:T(8,128)S(1)}, f32[4,3,64,256]{3,2,1,0:T(8,128)}, u32[]{:S(2)}) copy-start(f32[4,3,64,256]{3,2,1,0:T(8,128)} %gather_fusion.7) | copy-start | bytes 2359300
  112.2 142.2 %copy-start.4 = (f32[4,3,64,256]{3,2,1,0:T(8,128)S(1)}, f32[4,3,64,256]{3,2,1,0:T(8,128)}, u32[]{:S(2)}) copy-start(f32[4,3,64,256]{3,2,1,0:T(8,128)} %gather_fusion.5) | copy-start | bytes 2359300
  249.7 4.7 %copy-start.15 = (f32[4,64,256]{2,1,0:T(8,128)S(1)}, f32[4,64,256]{2,1,0:T(8,128)}, u32[]{:S(2)}) copy-start(f32[4,64,256]{2,1,0:T(8,128)} %get-tuple-element.40) | copy-start | bytes 786436
  296.2 20.6 %all-to-all-start.1 = ((f32[3,1,4,64,128]{4,2,0,1,3:T(4,128)}), f32[3,1,4,64,128]{4,2,0,1,3:T(4,128)S(1)}, u32[]{:S(2)}, u32[]{:S(2)}) async-start(f32[3,1,4,64,128]{4,2,0,1,3:T(4,128)} %reshape.459), calls=%async_computation.1 | async-start | bytes 786432 | tf_op jit(solution)/shard_map/all_to_all | solution.py:113
  (15 other events, 38.1 us)
Sparse Core Ops, SparseCore 0:
  18.9 76.5 all-reduce.2
  98.9 150.7 all-reduce.4
where the time goes:
time: 328 us; the launch traced here: 327 us
  waiting for transfers between devices  196 us (60%)
  local copies, waits for them, and re-layouts  50.8 us (15%)
  blocking collectives  27.5 us (8%)
  matrix products  17.6 us (5%)
  between operations  14.4 us (4%)
  starting transfers between devices  12.1 us (4%)
  other arithmetic  8.77 us (3%)
    psum x1, waiting for transfers between devices, local(): summed = lax.psum(stress, ('kx', 'real'))  134 us
    psum x1, waiting for transfers between devices, local(): low_fields = lax.psum(own_low, 'kx')  35.1 us
    all_to_all x1, blocking collectives, local(): lax.all_to_all(flat_out, ('kx', 'ht'), split_axis=3, concat_axis=3, tiled...  27.5 us
    all_to_all x1, waiting for transfers between devices, local(): lax.all_to_all(applied, ('kx', 'ht'), split_axis=3, concat_axis=3, tiled=...  14.2 us
    ppermute x1, waiting for transfers between devices, extended_2(): lax.ppermute(lax.slice_in_dim(block, block.shape[dim] - width, None, axis...  12.9 us
    gather x8, local copies, waits for them, and re-layouts, local(): partner = jnp.take(extended, local_partner[:, member], axis=2)  12 us
    unnamed x84, local copies, waits for them, and re-layouts  11.8 us
    slice x1, local copies, waits for them, and re-layouts, local(): low_one = low_fields[:, :, member:member + 1]  7.67 us
  transfers between devices with their start and end apart: 5, of which 4 were waited for; matrix products, arithmetic and copies ran while one was open for 15% of the time, Pallas kernels for 0%

commit v1 on v0

--- a/solution.py
+++ b/solution.py
@@ -88,7 +88,7 @@
         stresses.append(jnp.sum(weighted, axis=(1, 2)))
     stress = jnp.stack(stresses, axis=1)
     nonlinear = jnp.dot(high_low, backward, precision=highest)
-    summed = lax.psum(stress, ("kx", "real"))
+    summed = lax.psum(lax.psum(stress, "kx"), "real")
     low_forcing = jnp.dot(summed / realizations, backward, precision=highest)
     forcing = nonlinear * high_mask[None, None, :, None, None]
     forcing = (

time: 328 us -> 295 us (0.90)
  waiting for transfers between devices: 196 us -> 163 us
  other arithmetic: 8.77 us -> 21.4 us
  local copies, waits for them, and re-layouts: 50.8 us -> 40.4 us
    psum x1, waiting for transfers between devices: 134 us -> 44.3 us  [local(): summed = lax.psum(lax.psum(stress, 'kx'), 'real')]
    psum x1, waiting for transfers between devices: 35.1 us -> 91.8 us  [local(): low_fields = lax.psum(own_low, 'kx')]
    slice x1, local copies, waits for them, and re-layouts: 7.67 us -> 1.45 us  [local(): low_one = low_fields[:, :, member:member + 1]]
    select_n x16, other arithmetic: 3.58 us -> 9.24 us  [local(): partner = jnp.take(extended, local_partner[:, member], axis=2)]
    mul x1 -> x8, other arithmetic: 1.39 us -> 6.51 us  [local(): high_low = high_low + low_one * partner[1:2] + partner * low_one[1:2]]
    unnamed x84 -> x86, local copies, waits for them, and re-layouts: 11.8 us -> 11 us
  transfers between devices with their start and end apart: 5 -> 5, of which waited for: 4 -> 4; matrix products, arithmetic and copies ran while one was open for 15% -> 6% of each run, Pallas kernels for 0% -> 0%
where the time goes in v1:
time: 295 us
  waiting for transfers between devices  163 us (55%)
  local copies, waits for them, and re-layouts  40.4 us (14%)
  blocking collectives  25.8 us (9%)
  other arithmetic  21.4 us (7%)
  matrix products  17.8 us (6%)
  between operations  14.3 us (5%)
  starting transfers between devices  12.2 us (4%)
    psum x1, waiting for transfers between devices, local(): low_fields = lax.psum(own_low, 'kx')  91.8 us
    psum x1, waiting for transfers between devices, local(): summed = lax.psum(lax.psum(stress, 'kx'), 'real')  44.3 us
    all_to_all x1, blocking collectives, local(): lax.all_to_all(flat_out, ('kx', 'ht'), split_axis=3, concat_axis=3, tiled...  25.8 us
    all_to_all x1, waiting for transfers between devices, local(): lax.all_to_all(applied, ('kx', 'ht'), split_axis=3, concat_axis=3, tiled=...  14.2 us
    ppermute x1, waiting for transfers between devices, extended_2(): lax.ppermute(lax.slice_in_dim(block, block.shape[dim] - width, None, axis...  12.4 us
    gather x8, local copies, waits for them, and re-layouts, local(): partner = jnp.take(extended, local_partner[:, member], axis=2)  12 us
    unnamed x86, local copies, waits for them, and re-layouts  11 us
    select_n x16, other arithmetic, local(): partner = jnp.take(extended, local_partner[:, member], axis=2)  9.24 us
  transfers between devices with their start and end apart: 5, of which 4 were waited for; matrix products, arithmetic and copies ran while one was open for 6% of the time, Pallas kernels for 0%

profile of v1, /device:TPU:1, one launch (start us, length us, event | category | flops | bytes accessed | tf_op | source)
XLA Modules:
  0.0 294.6 jit_solution(11814889911047873270)
XLA Ops:
  6.6 2.4 fusion.12
  9.0 2.5 collective-permute-start
  11.6 4.0 %collective-permute-start.1 = (f32[3,1,4,64,256]{4,3,2,0,1:T(8,128)S(1)}, f32[3,1,4,64,256]{4,3,2,0,1:T(8,128)}, u32[]{:S(2)}, u32[]{:S(2)}) collective-permute-start(f32[3,1,4,64,256]{4,3,2,0,1:T(8,128)S(1)} %bitcast.259), channel_id=1, source_target_pairs={{32,0},{64,32},{96,64},{128,96},{160,128},{192,160},{224,192},{0,2... | collective-permute-start | bytes 2359304 | tf_op jit(solution)/shard_map/ppermute | solution.py:18
  17.0 3.2 %convolution_bitcast_fusion = f32[3,1,8,64,256]{4,2,3,0,1:T(8,128)} fusion(f32[3,4,64,256]{3,2,1,0:T(8,128)S(1)} %bitcast.260, s32[8]{0:T(128)} %param.11, s32[4]{0:T(128)S(1)} %get-tuple-element.58), kind=kOutput, calls=%fused_computation.14 | convolution fusion | flops 18874400 | bytes 2359344 | tf_op jit(solution)/shard_map/jm,crmyz->crjyz/dot_general | solution.py:79
  20.4 12.4 %collective-permute-done = f32[3,1,4,64,256]{4,3,2,0,1:T(8,128)S(1)} collective-permute-done((f32[3,1,4,64,256]{4,3,2,0,1:T(8,128)S(1)}, f32[3,1,4,64,256]{4,3,2,0,1:T(8,128)S(1)}, u32[]{:S(2)}, u32[]{:S(2)}) %collective-permute-start) | collective-permute-done | bytes 786464 | tf_op jit(solution)/shard_map/ppermute | solution.py:15
  33.6 1.8 maximum_bitcast_fusion
  35.4 1.6 gather_fusion
  37.0 1.5 gather_fusion.1
  41.6 1.5 gather_fusion.2
  45.2 1.5 gather_fusion.3
  48.8 1.5 gather_fusion.4
  52.4 1.5 gather_fusion.5
  56.0 1.5 gather_fusion.6
  59.6 1.5 gather_fusion.7
  63.3 1.6 multiply_reduce_fusion
  66.1 3.7 %stack.35 = f32[3,8,64,256]{3,1,2,0:T(8,128)} concatenate(f32[3,1,64,256]{3,1,2,0:T(1,128)S(1)} %stack.27, f32[3,1,64,256]{3,1,2,0:T(1,128)S(1)} %stack.28, f32[3,1,64,256]{3,1,2,0:T(1,128)S(1)} %stack.29, f32[3,1,64,256]{3,1,2,0:T(1,128)S(1)} %stack.30, f32[3,1,64,256]{3,1,2,0:T(1,128)S(1)} %stack.31, f32[3,1,64,256]{3,1,2,0:T(1,128)S(1)} %stack.32, ...), dimensions={1} | concatenate | bytes 3145728 | tf_op jit(solution)/shard_map/stack | solution.py:89
  70.1 91.8 %all-reduce.6.cloned.1.call-done = (f32[3,1,8,64,256]{4,2,3,0,1:T(8,128)}, f32[3,8,64,256]{3,1,2,0:T(8,128)}) async-done(((f32[3,1,8,64,256]{4,2,3,0,1:T(8,128)}, f32[3,8,64,256]{3,1,2,0:T(8,128)}), (f32[3,1,8,64,256]{4,2,3,0,1:T(8,128)}, f32[3,8,64,256]{3,1,2,0:T(8,128)})) %all-reduce.6.cloned.1.call-update) | async-done | bytes 3145744 | tf_op jit(solution)/shard_map/psum | solution.py:80
  174.4 44.3 %all-reduce.4.cloned.1.call-done = f32[3,8,64,256]{3,1,2,0:T(8,128)} async-done(((f32[3,8,64,256]{3,1,2,0:T(8,128)}), f32[3,8,64,256]{3,1,2,0:T(8,128)}) %all-reduce.4.cloned.1.call-update) | async-done | bytes 1572880 | tf_op jit(solution)/shard_map/psum | solution.py:91
  218.8 3.5 %fusion = f32[3,8,64,128]{3,1,2,0:T(8,128)S(1)} fusion(f32[3,8,64,256]{3,1,2,0:T(8,128)} %all-reduce.4.cloned.1.call-done, f32[256]{0:T(256)S(1)} %convert_multiply_fusion, f32[128]{0:T(128)} %copy-done.20, pred[128]{0:T(512)(128)(4,1)} %copy-done.19), kind=kOutput, calls=%fused_computation.12 | convolution fusion | flops 604504064 | bytes 2360960 | tf_op jit(solution)/shard_map/dot_general | solution.py:92
  223.5 6.1 %fusion.6 = f32[3,1,4,64,128]{4,3,2,0,1:T(8,128)} fusion(f32[3,1,4,64,128]{4,3,2,1,0:T(8,128)S(1)} %copy-done.10, f32[3,64,128,4]{2,3,1,0:T(4,128)S(1)} %fusion.50, f32[4,128]{1,0:T(4,128)S(1)} %compare_convert_fusion.1, f32[4]{0:T(128)S(1)} %broadcast_subtract_fusion, f32[256]{0:T(256)S(1)} %convert_multiply_fusion, f32[128]{0:T(128)} %copy-done.20, ...), kind=kOutput, calls=%fused_computation.21 | convolution fusion | flops 310280192 | bytes 11669168 | tf_op jit(solution)/shard_map/dot_general | solution.py:90
  233.7 25.8 %all_to_all.10 = f32[3,1,4,64,128]{4,2,0,1,3:T(4,128)S(1)} all-to-all(f32[3,1,4,64,128]{4,2,0,1,3:T(4,128)S(1)} %reshape.457), channel_id=1, replica_groups=mesh['kx'=8,'ht'=8,'real'=4] {'kx','ht'}, dimensions={3} | all-to-all | bytes 786432 | tf_op jit(solution)/shard_map/all_to_all | solution.py:106
  260.2 1.5 convolution_bitcast_fusion.1
  263.7 5.5 %all-to-all-start.1 = ((f32[3,1,4,64,128]{4,2,0,1,3:T(4,128)}), f32[3,1,4,64,128]{4,2,0,1,3:T(4,128)S(1)}, u32[]{:S(2)}, u32[]{:S(2)}) async-start(f32[3,1,4,64,128]{4,2,0,1,3:T(4,128)} %reshape.459), calls=%async_computation.1 | async-start | bytes 786432 | tf_op jit(solution)/shard_map/all_to_all | solution.py:113
  270.1 14.2 %all-to-all-done.1 = f32[3,1,4,64,128]{4,2,0,1,3:T(4,128)S(1)} async-done(((f32[3,1,4,64,128]{4,2,0,1,3:T(4,128)}), f32[3,1,4,64,128]{4,2,0,1,3:T(4,128)S(1)}, u32[]{:S(2)}, u32[]{:S(2)}) %all-to-all-start.1) | async-done | bytes 393248 | tf_op jit(solution)/shard_map/all_to_all | solution.py:113
  (178 shorter events, 44.1 us)
Async XLA Ops:
  6.5 253.7 %copy-start = (f32[1,512,512]{2,1,0:T(8,128)S(1)}, f32[1,512,512]{2,1,0:T(8,128)}, u32[]{:S(2)}) copy-start(f32[1,512,512]{2,1,0:T(8,128)} %param.15) | copy-start | bytes 3145732
  6.5 13.6 %copy-start.30 = (s32[8]{0:T(128)S(1)}, s32[8]{0:T(128)}, u32[]{:S(2)}) copy-start(s32[8]{0:T(128)} %param.11) | copy-start | bytes 100
  6.5 155.3 %all-reduce.6.cloned.1.call-start = ((), (), s32[]{:S(2)}) async-start(), calls=%async_computation.3 | async-start | bytes 6291456 | tf_op jit(solution)/shard_map/psum | solution.py:80
  9.0 23.7 %copy-start.1 = (f32[256,3,4,64]{0,3,2,1:T(8,128)}, f32[256,3,4,64]{0,3,2,1:T(8,128)S(1)}, u32[]{:S(2)}) copy-start(f32[256,3,4,64]{0,3,2,1:T(8,128)S(1)} %fusion.12) | copy-start | bytes 2359300
  9.0 23.7 %collective-permute-start = (f32[3,1,4,64,256]{4,3,2,0,1:T(8,128)S(1)}, f32[3,1,4,64,256]{4,3,2,0,1:T(8,128)S(1)}, u32[]{:S(2)}, u32[]{:S(2)}) collective-permute-start(f32[3,1,4,64,256]{4,3,2,0,1:T(8,128)S(1)} %bitcast.258), channel_id=1, source_target_pairs={{0,32},{32,64},{64,96},{96,128},{128,160},{160,192},{192,224},{224... | collective-permute-start | bytes 2359304 | tf_op jit(solution)/shard_map/ppermute | solution.py:15
  11.6 22.1 %collective-permute-start.1 = (f32[3,1,4,64,256]{4,3,2,0,1:T(8,128)S(1)}, f32[3,1,4,64,256]{4,3,2,0,1:T(8,128)}, u32[]{:S(2)}, u32[]{:S(2)}) collective-permute-start(f32[3,1,4,64,256]{4,3,2,0,1:T(8,128)S(1)} %bitcast.259), channel_id=1, source_target_pairs={{32,0},{64,32},{96,64},{128,96},{160,128},{192,160},{224,192},{0,2... | collective-permute-start | bytes 2359304 | tf_op jit(solution)/shard_map/ppermute | solution.py:18
  15.6 19.8 %copy-start.21 = (s32[4]{0:T(128)}, s32[4]{0:T(128)S(1)}, u32[]{:S(2)}) copy-start(s32[4]{0:T(128)S(1)} %get-tuple-element.58) | copy-start | bytes 52
  16.7 21.8 %copy-start.22 = (pred[4]{0:T(512)(128)(4,1)}, pred[4]{0:T(512)(128)(4,1)S(1)}, u32[]{:S(2)}) copy-start(pred[4]{0:T(512)(128)(4,1)S(1)} %compare_and_fusion.9) | copy-start | bytes 16
  16.7 23.9 %copy-start.23 = (pred[4]{0:T(512)(128)(4,1)}, pred[4]{0:T(512)(128)(4,1)S(1)}, u32[]{:S(2)}) copy-start(pred[4]{0:T(512)(128)(4,1)S(1)} %compare_and_fusion.8) | copy-start | bytes 16
  16.7 26.4 %copy-start.24 = (pred[4]{0:T(512)(128)(4,1)}, pred[4]{0:T(512)(128)(4,1)S(1)}, u32[]{:S(2)}) copy-start(pred[4]{0:T(512)(128)(4,1)S(1)} %compare_and_fusion.7) | copy-start | bytes 16
  16.8 29.9 %copy-start.25 = (pred[4]{0:T(512)(128)(4,1)}, pred[4]{0:T(512)(128)(4,1)S(1)}, u32[]{:S(2)}) copy-start(pred[4]{0:T(512)(128)(4,1)S(1)} %compare_and_fusion.6) | copy-start | bytes 16
  16.8 33.5 %copy-start.26 = (pred[4]{0:T(512)(128)(4,1)}, pred[4]{0:T(512)(128)(4,1)S(1)}, u32[]{:S(2)}) copy-start(pred[4]{0:T(512)(128)(4,1)S(1)} %compare_and_fusion.5) | copy-start | bytes 16
  16.9 37.0 %copy-start.27 = (pred[4]{0:T(512)(128)(4,1)}, pred[4]{0:T(512)(128)(4,1)S(1)}, u32[]{:S(2)}) copy-start(pred[4]{0:T(512)(128)(4,1)S(1)} %compare_and_fusion.4) | copy-start | bytes 16
  20.4 37.1 %copy-start.28 = (pred[4]{0:T(512)(128)(4,1)}, pred[4]{0:T(512)(128)(4,1)S(1)}, u32[]{:S(2)}) copy-start(pred[4]{0:T(512)(128)(4,1)S(1)} %compare_and_fusion.3) | copy-start | bytes 16
  20.4 40.7 %copy-start.29 = (pred[4]{0:T(512)(128)(4,1)}, pred[4]{0:T(512)(128)(4,1)S(1)}, u32[]{:S(2)}) copy-start(pred[4]{0:T(512)(128)(4,1)S(1)} %compare_and_fusion.2) | copy-start | bytes 16
  69.8 92.1 %copy-start.34 = (s32[64]{0:T(128)S(1)}, s32[64]{0:T(128)}, u32[]{:S(2)}) copy-start(s32[64]{0:T(128)} %param.13) | copy-start | bytes 772
  69.8 93.3 %copy-start.33 = (s32[4]{0:T(128)S(1)}, s32[4]{0:T(128)}, u32[]{:S(2)}) copy-start(s32[4]{0:T(128)} %param.14) | copy-start | bytes 52
  69.8 148.9 %all-reduce.4.cloned.1.call-start = ((), (), s32[]{:S(2)}) async-start(), calls=%async_computation.2 | async-start | bytes 3145728 | tf_op jit(solution)/shard_map/psum | solution.py:91
  170.6 52.8 %copy-start.3 = (f32[4,3,64,256]{3,2,1,0:T(8,128)S(1)}, f32[4,3,64,256]{3,2,1,0:T(8,128)}, u32[]{:S(2)}) copy-start(f32[4,3,64,256]{3,2,1,0:T(8,128)} %gather_fusion) | copy-start | bytes 2359300
  170.6 52.8 %copy-start.5 = (f32[4,3,64,256]{3,2,1,0:T(8,128)S(1)}, f32[4,3,64,256]{3,2,1,0:T(8,128)}, u32[]{:S(2)}) copy-start(f32[4,3,64,256]{3,2,1,0:T(8,128)} %gather_fusion.1) | copy-start | bytes 2359300
  170.7 52.8 %copy-start.6 = (f32[4,3,64,256]{3,2,1,0:T(8,128)S(1)}, f32[4,3,64,256]{3,2,1,0:T(8,128)}, u32[]{:S(2)}) copy-start(f32[4,3,64,256]{3,2,1,0:T(8,128)} %gather_fusion.2) | copy-start | bytes 2359300
  218.8 4.7 %copy-start.10 = (f32[3,1,4,64,128]{4,3,2,1,0:T(8,128)S(1)}, f32[3,1,4,64,128]{4,3,2,1,0:T(8,128)}, u32[]{:S(2)}) copy-start(f32[3,1,4,64,128]{4,3,2,1,0:T(8,128)} %param.10) | copy-start | bytes 1179652
  218.8 4.7 %copy-start.11 = (f32[4,64,256]{2,1,0:T(8,128)S(1)}, f32[4,64,256]{2,1,0:T(8,128)}, u32[]{:S(2)}) copy-start(f32[4,64,256]{2,1,0:T(8,128)} %get-tuple-element.41) | copy-start | bytes 786436
  263.7 20.6 %all-to-all-start.1 = ((f32[3,1,4,64,128]{4,2,0,1,3:T(4,128)}), f32[3,1,4,64,128]{4,2,0,1,3:T(4,128)S(1)}, u32[]{:S(2)}, u32[]{:S(2)}) async-start(f32[3,1,4,64,128]{4,2,0,1,3:T(4,128)} %reshape.459), calls=%async_computation.1 | async-start | bytes 786432 | tf_op jit(solution)/shard_map/all_to_all | solution.py:113
  (16 other events, 35.7 us)
Sparse Core Ops, SparseCore 0:
  70.0 91.8 all-reduce.5
  164.2 54.4 all-reduce.3
